TPU v7x, 32 devices: a whole 2x2x4 slice. The times are simulated.
32 devices in a mesh: group: 2 (over x), replica: 16 (over z, y, core).
Axes of the slice: x: 2, y: 2, z: 4, core: 2. Of those that a mesh axis runs over, the one named last changes fastest.
Arguments:
- tokens: bfloat16 [32, 1024, 768], P(('group', 'replica')), may hold values from -6 to 6
- lengths: int32 [32], P(('group', 'replica')), may hold values from 256 to 1024, as said below
- w_qkv: bfloat16 [768, 2304], P('group'), may hold values from -0.21875 to 0.21875
- w_out: bfloat16 [768, 768], P('group'), may hold values from -4 to 4
- gain_one: bfloat16 [768], P('group'), may hold values from 0.25 to 1.75
- w_in: bfloat16 [768, 2304], P('group'), may hold values from -0.21875 to 0.21875
- w_down: bfloat16 [1152, 768], P('group'), may hold values from -0.1875 to 0.1875
- gain_two: bfloat16 [768], P('group'), may hold values from 0.25 to 1.75
- cotangent: bfloat16 [32, 1024, 768], P(('group', 'replica')), may hold values from -6 to 6
Outputs:
- output: bfloat16 [32, 1024, 768], P(('group', 'replica'))
- grad_tokens: float32 [32, 1024, 768], P(('group', 'replica'))
- grad_qkv: float32 [768, 2304], P('group')
- grad_out: float32 [768, 768], P('group')
- grad_gain_one: float32 [768], P('group')
- grad_in: float32 [768, 2304], P('group')
- grad_down: float32 [1152, 768], P('group')
- grad_gain_two: float32 [768], P('group')
Inputs may be any that keep to these rules, and one draw needn't show every extreme that they name: Slots 0 to lengths - 1 of a sequence hold tokens, the rest are padding; some sequence has exactly 1024 valid slots and some exactly 256.
All inputs are finite; a program needn't handle non-finite values.
Results may differ from a plain program's by a relative error of at most 0.018.
Values may be sent and summed in bfloat16 or wider, within the bound.
No kernel may reach another device: no remote copies, remote signals or barrier semaphores. Data moves between devices by JAX's collectives and lax.ppermute only.
A program may use at most 192 MiB of HBM per device.

v0:
```python
import math
import jax
import jax.numpy as jnp
from jax import lax
from jax.sharding import PartitionSpec as P

HEADS = 12
HEAD_DIM = 64
theta_base = 160000.0
norm_eps = 1e-05


def normed(field, gain):
    center = field - jnp.mean(field, axis=-1, keepdims=True)
    spread = jnp.mean(center * center, axis=-1, keepdims=True)
    return center * lax.rsqrt(spread + norm_eps) * gain


def rotary(field):
    half = HEAD_DIM // 2
    length = field.shape[1]
    freq = jnp.exp(-math.log(theta_base) * 2.0 * jnp.arange(half, dtype=jnp.float32) / HEAD_DIM)
    angle = jnp.arange(length, dtype=jnp.float32)[:, None] * freq[None, :]
    cosine = jnp.cos(angle)
    sine = jnp.sin(angle)
    first = field[..., :half]
    second = field[..., half:]
    return jnp.concatenate(
        [first * cosine - second * sine, second * cosine + first * sine], axis=-1
    )


def rotate_both(query, key_rows):
    return (rotary(query), rotary(key_rows))


def geglu(upward):
    half = upward.shape[1] // 2
    return jax.nn.gelu(upward[:, :half], approximate=False) * upward[:, half:]


def inner(left, right):
    return lax.dot_general(
        left, right, (((0,), (0,)), ((), ())), preferred_element_type=jnp.float32
    )


def outer(left, right):
    return lax.dot_general(
        left, right, (((1,), (1,)), ((), ())), preferred_element_type=jnp.float32
    )


def swap_replica(field, bit):
    count = lax.axis_size("replica")
    return lax.ppermute(field, "replica", [(i, i ^ bit) for i in range(count)])


def swap_group(field):
    return lax.ppermute(field, "group", [(0, 1), (1, 0)])


def pick(field, index, axis):
    size = field.shape[axis] // 2
    return lax.dynamic_slice_in_dim(field, index * size, size, axis)


def in_order(mine, other, index, axis):
    return jnp.where(
        index == 0,
        jnp.concatenate([mine, other], axis=axis),
        jnp.concatenate([other, mine], axis=axis),
    )


def add_low(left, right):
    return (left.astype(jnp.float32) + right.astype(jnp.float32)).astype(jnp.bfloat16)


def other_rows(send, core):
    fetched = swap_group(send)
    return (fetched, swap_replica(fetched, 1))


def reduce_unit(send, keep, group, replica):
    count = lax.axis_size("replica")
    total = add_low(keep, swap_replica(send, 1))
    total = add_low(pick(total, group, 0), swap_group(pick(total, 1 - group, 0)))[0]
    split = []
    bit = 2
    while bit < count:
        at = replica // bit % 2
        if total.shape[0] % 32 == 0:
            total = add_low(pick(total, at, 0), swap_replica(pick(total, 1 - at, 0), bit))
            split.append((bit, at))
        else:
            total = add_low(total, swap_replica(total, bit))
        bit *= 2
    for bit, at in reversed(split):
        total = in_order(total, swap_replica(total, bit), at, 0)
    return (total, swap_replica(total, 1))


def on_device(tokens, lengths, w_qkv, w_out, gain_one, w_in, w_down, gain_two, cotangent):
    field = tokens[0].astype(jnp.float32)
    length = field.shape[0]
    width = field.shape[1]
    scale = 1.0 / math.sqrt(HEAD_DIM)
    valid = jnp.arange(length, dtype=jnp.int32) < lengths[0]
    group = lax.axis_index("group")
    replica = lax.axis_index("replica")
    core = replica % 2
    gain_rows = jnp.zeros((16, w_qkv.shape[1] // 2), jnp.bfloat16)
    gain_rows = lax.dynamic_update_slice(gain_rows, gain_one[None], (0, 0))
    qkv_send = jnp.concatenate([pick(w_qkv, core, 1), gain_rows], axis=0)
    rest_rows = jnp.zeros((16, w_out.shape[1] // 2), jnp.bfloat16)
    rest_rows = lax.dynamic_update_slice(rest_rows, gain_two[None], (0, 0))
    wide = w_out.shape[1] // 2
    in_half = pick(w_in, core, 1)
    rest_send = jnp.concatenate(
        [pick(w_out, core, 1), pick(w_down, core, 1)]
        + [in_half[:, i * wide : (i + 1) * wide] for i in range(3)]
        + [rest_rows],
        axis=0,
    )
    qkv_parts = other_rows(qkv_send, core)
    rest_parts = other_rows(rest_send, core)
    n_own = w_qkv.shape[0]
    n_down = w_down.shape[0]
    cut = [0, n_own, n_own + n_down, 2 * n_own + n_down, 3 * n_own + n_down, 4 * n_own + n_down]

    def whole(own, parts):
        return in_order(own, in_order(parts[0], parts[1], core, 1), group, 0)

    qkv_full = whole(w_qkv, [part[:n_own] for part in qkv_parts])
    gain_first = in_order(gain_one, qkv_parts[0][n_own, :n_own], group, 0)
    out_full = whole(w_out, [part[: cut[1]] for part in rest_parts])
    down_full = whole(w_down, [part[cut[1] : cut[2]] for part in rest_parts])
    in_full = whole(
        w_in,
        [
            jnp.concatenate([part[cut[i] : cut[i + 1]] for i in (2, 3, 4)], axis=1)
            for part in rest_parts
        ],
    )
    gain_second = in_order(gain_two, rest_parts[0][cut[5], :n_own], group, 0)
    first_f, first_pull = jax.vjp(normed, field, gain_first.astype(jnp.float32))
    first_in = first_f.astype(jnp.bfloat16)
    merged = jnp.dot(first_in, qkv_full, preferred_element_type=jnp.float32)
    parts = merged.reshape(length, 3, HEADS, HEAD_DIM).transpose(1, 2, 0, 3)
    (query_f, key_f), rotate_pull = jax.vjp(rotate_both, parts[0], parts[1])
    query = query_f.astype(jnp.bfloat16)
    key_rows = key_f.astype(jnp.bfloat16)
    values = parts[2].astype(jnp.bfloat16)

    def masked_scores(head_query, head_keys):
        scores = (
            jnp.einsum("qd,kd->qk", head_query, head_keys, preferred_element_type=jnp.float32)
            * scale
        )
        return jnp.where(valid[None, :], scores, -1e30)

    def forward_head(item):
        head_query, head_keys, head_values = item
        scores = masked_scores(head_query, head_keys)
        top = jnp.max(scores, axis=1, keepdims=True)
        weights = jnp.exp(scores - top)
        total = jnp.sum(weights, axis=1, keepdims=True)
        weights = weights / total
        result = jnp.einsum(
            "qk,kd->qd",
            weights.astype(jnp.bfloat16),
            head_values,
            preferred_element_type=jnp.float32,
        )
        return (result, top[:, 0] + jnp.log(total[:, 0]))

    heads, log_totals = lax.map(forward_head, (query, key_rows, values))
    mixed = heads.transpose(1, 0, 2).reshape(length, width).astype(jnp.bfloat16)
    middle = field + jnp.dot(mixed, out_full, preferred_element_type=jnp.float32)
    second_f, second_pull = jax.vjp(normed, middle, gain_second.astype(jnp.float32))
    second_in = second_f.astype(jnp.bfloat16)
    upward = jnp.dot(second_in, in_full, preferred_element_type=jnp.float32)
    activ_f, activ_pull = jax.vjp(geglu, upward)
    activ = activ_f.astype(jnp.bfloat16)
    result = middle + jnp.dot(activ, down_full, preferred_element_type=jnp.float32)
    output = jnp.where(valid[:, None], result, 0.0).astype(jnp.bfloat16)[None]
    d_out = jnp.where(valid[:, None], cotangent[0], jnp.zeros((), jnp.bfloat16))
    grad_down = inner(activ, d_out)
    d_activ = outer(d_out, down_full)
    (d_up,) = activ_pull(d_activ)
    d_up = d_up.astype(jnp.bfloat16)
    grad_in = inner(second_in, d_up)
    d_second = outer(d_up, in_full)
    d_middle_norm, grad_gain_two = second_pull(d_second)
    d_middle = d_out.astype(jnp.float32) + d_middle_norm
    d_middle_low = d_middle.astype(jnp.bfloat16)
    grad_out = inner(mixed, d_middle_low)
    d_mixed = outer(d_middle_low, out_full).astype(jnp.bfloat16)
    d_heads = d_mixed.reshape(length, HEADS, HEAD_DIM).transpose(1, 0, 2)

    def backward_head(item):
        head_query, head_keys, head_values, head_grad, log_total = item
        scores = masked_scores(head_query, head_keys)
        weights = jnp.where(valid[None, :], jnp.exp(scores - log_total[:, None]), 0.0)
        d_values = jnp.einsum(
            "qk,qd->kd", weights.astype(jnp.bfloat16), head_grad, preferred_element_type=jnp.float32
        )
        d_weights = jnp.einsum(
            "qd,kd->qk", head_grad, head_values, preferred_element_type=jnp.float32
        )
        d_scores = weights * (d_weights - jnp.sum(weights * d_weights, axis=1, keepdims=True))
        d_scores = d_scores.astype(jnp.bfloat16)
        d_query = (
            jnp.einsum("qk,kd->qd", d_scores, head_keys, preferred_element_type=jnp.float32) * scale
        )
        d_keys = (
            jnp.einsum("qk,qd->kd", d_scores, head_query, preferred_element_type=jnp.float32)
            * scale
        )
        return (d_query, d_keys, d_values)

    d_query_r, d_keys_r, d_values = lax.map(
        backward_head, (query, key_rows, values, d_heads, log_totals)
    )
    d_query, d_keys = rotate_pull((d_query_r, d_keys_r))
    d_merged = (
        jnp.stack([d_query, d_keys, d_values]).transpose(2, 0, 1, 3).reshape(length, 3 * width)
    )
    d_merged = d_merged.astype(jnp.bfloat16)
    grad_qkv = inner(first_in, d_merged)
    d_first = outer(d_merged, qkv_full)
    d_field_norm, grad_gain_one = first_pull(d_first)
    grad_tokens = (d_middle + d_field_norm)[None]

    def unit_of(fields):
        halves = []
        for half in (1 - core, core):
            parts = []
            for field in fields:
                part = pick(field.astype(jnp.bfloat16), half, 1)
                rows = part.shape[0] // 2
                for i in range(part.shape[1] // wide):
                    parts.append(part[:, i * wide : (i + 1) * wide].reshape(2, rows, wide))
            used = sum((part.shape[1] for part in parts))
            filled = -(-used // 128) * 128
            if filled > used:
                parts.append(jnp.zeros((2, filled - used, wide), jnp.bfloat16))
            halves.append(jnp.concatenate(parts, axis=1))
        return halves

    def gain_unit(field):
        return (
            jnp.zeros((2 * n_own, 2 * wide), jnp.float32)
            .at[:2, :n_own]
            .set(field.reshape(2, n_own))
        )

    def spread(result, fields):
        outs = []
        at = 0
        for field in fields:
            rows = field.shape[0] // 2
            count = field.shape[1] // 2 // wide
            sides = []
            for side in result:
                sides.append(
                    jnp.concatenate(
                        [side[at + i * rows : at + (i + 1) * rows] for i in range(count)], axis=1
                    )
                )
            outs.append(in_order(sides[0], sides[1], core, 1).astype(jnp.float32))
            at += rows * count
        return outs

    early = [grad_down, grad_in, grad_out]
    early_sum = reduce_unit(*unit_of(early), group, replica)
    late = [grad_qkv]
    late_sum = reduce_unit(*unit_of(late), group, replica)
    grad_down, grad_in, grad_out = spread(early_sum, early)
    (grad_qkv,) = spread(late_sum, late)
    gains = jnp.stack([grad_gain_one, grad_gain_two])
    gains = lax.psum(gains, ("group", "replica"))
    gains = lax.dynamic_slice_in_dim(gains, group * n_own, n_own, 1)
    return (output, grad_tokens, grad_qkv, grad_out, gains[0], grad_in, grad_down, gains[1])


def solution(mesh):
    in_specs = (
        P(("group", "replica"), None, None),
        P(("group", "replica")),
        P("group", None),
        P("group", None),
        P("group"),
        P("group", None),
        P("group", None),
        P("group"),
        P(("group", "replica"), None, None),
    )
    out_specs = (
        P(("group", "replica"), None, None),
        P(("group", "replica"), None, None),
        P("group", None),
        P("group", None),
        P("group"),
        P("group", None),
        P("group", None),
        P("group"),
    )
    return jax.shard_map(
        on_device, mesh=mesh, in_specs=in_specs, out_specs=out_specs, check_vma=False
    )
```

profile of v0, /device:TPU:1, one launch (start us, length us, event | category | flops | bytes accessed | tf_op | source)
XLA Modules:
  0.0 799.1 jit_solution(9865017861474288771)
XLA Ops:
  11.8 4.3 copy.179
  34.1 27.3 %collective-permute-done.2 = bf16[2128,384]{1,0:T(8,128)(2,1)} collective-permute-done((bf16[2128,384]{1,0:T(8,128)(2,1)}, bf16[2128,384]{1,0:T(8,128)(2,1)}, u32[]{:S(2)}, u32[]{:S(2)}) %collective-permute-start.2) | collective-permute-done | bytes 1634336 | tf_op jit(solution)/shard_map/ppermute | solution.py:60
  96.5 4.3 copy.184
  100.8 123.5 %while.30 = (s32[]{:T(128)}, bf16[12,1024,64]{1,2,0:T(8,128)(2,1)S(1)}, f32[12,1024]{1,0:T(8,128)}, bf16[12,1024,64]{2,1,0:T(8,128)(2,1)}, bf16[12,1024,64]{2,1,...) while((s32[]{:T(128)}, bf16[12,1024,64]{1,2,0:T(8,128)(2,1)S(1)}, ...), condition=%wide.region_5.6_spmd.clone.clone, body=%wide.region_2.5_spmd.clone.sunk.clone | while | flops 281018368 | bytes 30455920 | solution.py:178
  247.4 4.3 fusion.87
  251.7 14.9 %fusion.78 = (f32[1024,1152]{1,0:T(8,128)}, f32[1024,1152]{1,0:T(8,128)S(1)}, f32[1024,1152]{1,0:T(8,128)S(1)}) fusion(f32[1024,2304]{1,0:T(8,128)S(1)} %fusion.87, bf16[576,768]{0,1:T(8,128)(2,1)S(1)} %maximum_select_fusion.6, bf16[576,768]{0,1:T(8,128)(2,1)S(1)} %copy-done.44, pred[]{:T(512)S(6)} %eq.18, bf16[1,1024,768]{1,2,0:T(8,128)(2,1)S(1)} %copy-done.8, ...), kind=kOutput, calls=%fused_computation.147 | convolution fusion | flops 1897365504 | bytes 22217728 | tf_op jit(solution)/shard_map/dot_general | solution.py:49
  266.7 4.5 multiply_add_fusion
  271.2 11.5 %multiply_reduce_fusion.1 = (f32[768]{0:T(1024)}, f32[1024]{0:T(1024)S(1)}, f32[1024,768]{0,1:T(8,128)}) fusion(f32[1024,768]{0,1:T(8,128)S(1)} %copy-done.13, f32[1024]{0:T(1024)S(1)} %fusion.95, f32[1024]{0:T(1024)S(1)} %broadcast_multiply_fusion, f32[768]{0:T(1024)S(1)} %fusion.97, bf16[384,2304]{0,1:T(8,128)(2,1)} %copy-done.32, ...), kind=kOutput, calls=%fused_computation.109 | convolution fusion | flops 3650025728 | bytes 19286016 | tf_op jit(solution)/shard_map/dot_general | solution.py:49
  282.7 9.6 %convolution_convert_fusion = bf16[768,2304]{1,0:T(8,128)(2,1)} fusion(f32[1024,1152]{1,0:T(8,128)} %get-tuple-element.318, f32[1024,1152]{1,0:T(8,128)} %get-tuple-element.312, f32[1024,768]{0,1:T(8,128)S(1)} %copy-done.13, f32[768]{0:T(1024)S(1)} %fusion.97, f32[1024]{0:T(1024)S(1)} %fusion.95, f32[1024]{0:T(1024)S(1)} %broadcast_multiply_fusion), kind=kOutput, calls=%fused_computation.62 | convolution fusion | flops 3633512448 | bytes 16133120 | tf_op jit(solution)/shard_map/dot_general | solution.py:43
  298.0 4.2 copy.203
  302.2 160.5 %while.31 = (s32[]{:T(128)}, f32[12,1024,64]{1,2,0:T(8,128)}, f32[12,1024,64]{1,2,0:T(8,128)}, bf16[12,1024,64]{1,2,0:T(8,128)(2,1)S(1)}, bf16[12,1024,64]{2,1,0...) while((s32[]{:T(128)}, f32[12,1024,64]{1,2,0:T(8,128)}, ...), condition=%wide.region_12.13_spmd.clone.clone, body=%wide.region_10.12_spmd.clone.sunk.clone | while | flops 681705472 | bytes 34106476 | solution.py:223
  467.8 4.8 convolution_convert_fusion.1
  503.5 6.9 concatenate.218
  523.2 19.9 %collective-permute-done.5 = bf16[1,1152,384]{1,2,0:T(8,128)(2,1)} collective-permute-done((bf16[1,1152,384]{1,2,0:T(8,128)(2,1)}, bf16[1,1152,384]{1,2,0:T(8,128)(2,1)}, u32[]{:S(2)}, u32[]{:S(2)}) %collective-permute-start.5) | collective-permute-done | bytes 884768 | tf_op jit(solution)/shard_map/ppermute | solution.py:60
  559.0 7.1 concatenate.217
  581.5 9.8 %fusion.66 = (f32[1024]{0:T(1024)}, f32[1024,768]{0,1:T(8,128)}) fusion(bf16[1,1024,768]{1,2,0:T(8,128)(2,1)S(1)} %copy.176, f32[768]{0:T(1024)S(1)} %copy-done.54, f32[1024]{0:T(1024)S(1)} %copy-done.50, bf16[1024,2304]{0,1:T(8,128)(2,1)} %bitcast.224, bf16[768,2304]{0,1:T(8,128)(2,1)} %copy-done.21), kind=kOutput, calls=%fused_computation.100 | convolution fusion | flops 3627809792 | bytes 12987392 | tf_op jit(solution)/shard_map/dot_general | solution.py:49
  591.7 21.8 %collective-permute-done.14 = bf16[1,2176,384]{1,2,0:T(8,128)(2,1)} collective-permute-done((bf16[1,2176,384]{1,2,0:T(8,128)(2,1)}, bf16[1,2176,384]{1,2,0:T(8,128)(2,1)}, u32[]{:S(2)}, u32[]{:S(2)}) %collective-permute-start.14) | collective-permute-done | bytes 1671200 | tf_op jit(solution)/shard_map/ppermute | solution.py:60
  620.2 7.1 fusion.79
  627.8 5.9 collective-permute-done.10
  644.4 6.6 collective-permute-done.16
  656.5 10.4 %collective-permute-start.12 = (bf16[1152,384]{0,1:T(8,128)(2,1)}, bf16[1152,384]{0,1:T(8,128)(2,1)}, u32[]{:S(2)}, u32[]{:S(2)}) collective-permute-start(bf16[1152,384]{0,1:T(8,128)(2,1)} %maximum_select_fusion.8), channel_id=1, source_target_pairs={{0,1},{1,0},{2,3},{3,2},{4,5},{5,4},{6,7},{7,6},{8,9},{9,8},{10,11... | collective-permute-start | bytes 2654216 | tf_op jit(solution)/shard_map/ppermute | solution.py:56
  667.2 9.3 %collective-permute-done.18 = bf16[272,384]{0,1:T(8,128)(2,1)S(1)} collective-permute-done((bf16[272,384]{0,1:T(8,128)(2,1)S(1)}, bf16[272,384]{0,1:T(8,128)(2,1)S(1)}, u32[]{:S(2)}, u32[]{:S(2)}) %collective-permute-start.18) | collective-permute-done | bytes 208928 | tf_op jit(solution)/shard_map/ppermute | solution.py:56
  686.3 47.6 %psum.7 = f32[2,768]{1,0:T(2,128)S(1)} all-reduce(f32[2,768]{1,0:T(2,128)S(1)} %pad_maximum_fusion.3), channel_id=1, replica_groups=mesh['group'=2,'replica'=16] {'group','replica'}, use_global_device_ids=true, to_apply=%region_17.18 | all-reduce | flops 1536 | bytes 12288 | tf_op jit(solution)/shard_map/psum | solution.py:283
  748.8 10.8 %collective-permute-done.20 = bf16[1088,384]{1,0:T(8,128)(2,1)} collective-permute-done((bf16[1088,384]{1,0:T(8,128)(2,1)S(1)}, bf16[1088,384]{1,0:T(8,128)(2,1)}, u32[]{:S(2)}, u32[]{:S(2)}) %collective-permute-start.20) | collective-permute-done | bytes 835616 | tf_op jit(solution)/shard_map/ppermute | solution.py:56
  (526 shorter events, 542.0 us)
Async XLA Ops:
  3.9 25.9 %collective-permute-start = (bf16[400,1152]{1,0:T(8,128)(2,1)}, bf16[400,1152]{1,0:T(8,128)(2,1)}, u32[]{:S(2)}, u32[]{:S(2)}) collective-permute-start(bf16[400,1152]{1,0:T(8,128)(2,1)} %fusion.83), channel_id=1, source_target_pairs={{0,16},{16,0},{1,17},{17,1},{2,18},{18,2},{3,19},{19,3},{4,20},{20... | collective-permute-start | bytes 2764808 | tf_op jit(solution)/shard_map/ppermute | solution.py:60
  10.3 51.1 %collective-permute-start.2 = (bf16[2128,384]{1,0:T(8,128)(2,1)}, bf16[2128,384]{1,0:T(8,128)(2,1)}, u32[]{:S(2)}, u32[]{:S(2)}) collective-permute-start(bf16[2128,384]{1,0:T(8,128)(2,1)} %constant_dynamic-update-slice_fusion), channel_id=1, source_target_pairs={{0,16},{16,0},{1,17},{17,1},{2,18},{18,2},{3,19},{19,3},{4,20},{20... | collective-permute-start | bytes 4902920 | tf_op jit(solution)/shard_map/ppermute | solution.py:60
  29.8 40.7 %collective-permute-start.1 = (bf16[400,1152]{1,0:T(8,128)(2,1)}, bf16[400,1152]{1,0:T(8,128)(2,1)}, u32[]{:S(2)}, u32[]{:S(2)}) collective-permute-start(bf16[400,1152]{1,0:T(8,128)(2,1)} %collective-permute-done), channel_id=1, source_target_pairs={{0,1},{1,0},{2,3},{3,2},{4,5},{5,4},{6,7},{7,6},{8,9},{9,8},{10,11... | collective-permute-start | bytes 2764808 | tf_op jit(solution)/shard_map/ppermute | solution.py:56
  68.5 155.8 %collective-permute-start.3 = (bf16[2128,384]{1,0:T(8,128)(2,1)}, bf16[2128,384]{1,0:T(8,128)(2,1)}, u32[]{:S(2)}, u32[]{:S(2)}) collective-permute-start(bf16[2128,384]{1,0:T(8,128)(2,1)} %collective-permute-done.2), channel_id=1, source_target_pairs={{0,1},{1,0},{2,3},{3,2},{4,5},{5,4},{6,7},{7,6},{8,9},{9,8},{10,11... | collective-permute-start | bytes 4902920 | tf_op jit(solution)/shard_map/ppermute | solution.py:56
  302.2 160.5 %copy-start.37 = (f32[1024,32]{0,1:T(8,128)S(1)}, f32[1024,32]{0,1:T(8,128)}, u32[]{:S(2)}) copy-start(f32[1024,32]{0,1:T(8,128)} %copy-done.36) | copy-start | bytes 393220
  302.2 160.5 %copy-start.39 = (f32[1024,32]{0,1:T(8,128)S(1)}, f32[1024,32]{0,1:T(8,128)}, u32[]{:S(2)}) copy-start(f32[1024,32]{0,1:T(8,128)} %get-tuple-element.382) | copy-start | bytes 393220
  483.6 33.6 %collective-permute-start.4 = (bf16[2,1152,384]{1,2,0:T(8,128)(2,1)}, bf16[2,1152,384]{1,2,0:T(8,128)(2,1)}, u32[]{:S(2)}, u32[]{:S(2)}) collective-permute-start(bf16[2,1152,384]{1,2,0:T(8,128)(2,1)} %pad_maximum_fusion), channel_id=1, source_target_pairs={{0,1},{1,0},{2,3},{3,2},{4,5},{5,4},{6,7},{7,6},{8,9},{9,8},{10,11... | collective-permute-start | bytes 5308424 | tf_op jit(solution)/shard_map/ppermute | solution.py:56
  510.5 59.4 %collective-permute-start.13 = (bf16[2,2176,384]{1,2,0:T(8,128)(2,1)}, bf16[2,2176,384]{1,2,0:T(8,128)(2,1)}, u32[]{:S(2)}, u32[]{:S(2)}) collective-permute-start(bf16[2,2176,384]{1,2,0:T(8,128)(2,1)} %concatenate.218), channel_id=1, source_target_pairs={{0,1},{1,0},{2,3},{3,2},{4,5},{5,4},{6,7},{7,6},{8,9},{9,8},{10,11... | collective-permute-start | bytes 10027016 | tf_op jit(solution)/shard_map/ppermute | solution.py:56
  521.8 21.4 %collective-permute-start.5 = (bf16[1,1152,384]{1,2,0:T(8,128)(2,1)}, bf16[1,1152,384]{1,2,0:T(8,128)(2,1)}, u32[]{:S(2)}, u32[]{:S(2)}) collective-permute-start(bf16[1,1152,384]{1,2,0:T(8,128)(2,1)} %constant_dynamic-slice_fusion.22), channel_id=1, source_target_pairs={{0,16},{16,0},{1,17},{17,1},{2,18},{18,2},{3,19},{19,3},{4,20},{20... | collective-permute-start | bytes 2654216 | tf_op jit(solution)/shard_map/ppermute | solution.py:60
  546.7 19.4 %collective-permute-start.6 = (bf16[576,384]{0,1:T(8,128)(2,1)}, bf16[576,384]{0,1:T(8,128)(2,1)}, u32[]{:S(2)}, u32[]{:S(2)}) collective-permute-start(bf16[576,384]{0,1:T(8,128)(2,1)} %dynamic-slice_bitcast_fusion), channel_id=1, source_target_pairs={{0,2},{1,3},{2,0},{3,1},{4,6},{5,7},{6,4},{7,5},{8,10},{9,11},{10,... | collective-permute-start | bytes 1327112 | tf_op jit(solution)/shard_map/ppermute | solution.py:56
  568.6 9.3 %collective-permute-start.7 = (bf16[288,384]{0,1:T(8,128)(2,1)}, bf16[288,384]{0,1:T(8,128)(2,1)S(1)}, u32[]{:S(2)}, u32[]{:S(2)}) collective-permute-start(bf16[288,384]{0,1:T(8,128)(2,1)} %constant_dynamic-slice_fusion.21), channel_id=1, source_target_pairs={{0,4},{1,5},{2,6},{3,7},{4,0},{5,1},{6,2},{7,3},{8,12},{9,13},{10,... | collective-permute-start | bytes 663560 | tf_op jit(solution)/shard_map/ppermute | solution.py:56
  576.6 36.8 %collective-permute-start.14 = (bf16[1,2176,384]{1,2,0:T(8,128)(2,1)}, bf16[1,2176,384]{1,2,0:T(8,128)(2,1)}, u32[]{:S(2)}, u32[]{:S(2)}) collective-permute-start(bf16[1,2176,384]{1,2,0:T(8,128)(2,1)} %constant_dynamic-slice_fusion.13), channel_id=1, source_target_pairs={{0,16},{16,0},{1,17},{17,1},{2,18},{18,2},{3,19},{19,3},{4,20},{20... | collective-permute-start | bytes 5013512 | tf_op jit(solution)/shard_map/ppermute | solution.py:60
  579.1 12.2 %collective-permute-start.8 = (bf16[144,384]{0,1:T(8,128)(2,1)S(1)}, bf16[144,384]{0,1:T(8,128)(2,1)S(1)}, u32[]{:S(2)}, u32[]{:S(2)}) collective-permute-start(bf16[144,384]{0,1:T(8,128)(2,1)S(1)} %constant_dynamic-slice_fusion.20), channel_id=1, source_target_pairs={{0,8},{1,9},{2,10},{3,11},{4,12},{5,13},{6,14},{7,15},{8,0},{9,1},... | collective-permute-start | bytes 331784 | tf_op jit(solution)/shard_map/ppermute | solution.py:56
  591.5 35.9 %collective-permute-start.9 = (bf16[144,384]{0,1:T(8,128)(2,1)S(1)}, bf16[144,384]{0,1:T(8,128)(2,1)S(1)}, u32[]{:S(2)}, u32[]{:S(2)}) collective-permute-start(bf16[144,384]{0,1:T(8,128)(2,1)S(1)} %add_convert_fusion.12), channel_id=1, source_target_pairs={{0,8},{1,9},{2,10},{3,11},{4,12},{5,13},{6,14},{7,15},{8,0},{9,1},... | collective-permute-start | bytes 331784 | tf_op jit(solution)/shard_map/ppermute | solution.py:56
  620.0 18.1 %collective-permute-start.15 = (bf16[1088,384]{1,0:T(8,128)(2,1)}, bf16[1088,384]{1,0:T(8,128)(2,1)}, u32[]{:S(2)}, u32[]{:S(2)}) collective-permute-start(bf16[1088,384]{1,0:T(8,128)(2,1)} %bitcast.243), channel_id=1, source_target_pairs={{0,2},{1,3},{2,0},{3,1},{4,6},{5,7},{6,4},{7,5},{8,10},{9,11},{10,... | collective-permute-start | bytes 2506760 | tf_op jit(solution)/shard_map/ppermute | solution.py:56
  627.6 6.0 collective-permute-start.10
  634.8 18.8 %collective-permute-start.11 = (bf16[576,384]{0,1:T(8,128)(2,1)}, bf16[576,384]{0,1:T(8,128)(2,1)}, u32[]{:S(2)}, u32[]{:S(2)}) collective-permute-start(bf16[576,384]{0,1:T(8,128)(2,1)} %maximum_select_fusion.14), channel_id=1, source_target_pairs={{0,2},{1,3},{2,0},{3,1},{4,6},{5,7},{6,4},{7,5},{8,10},{9,11},{10,... | collective-permute-start | bytes 1327112 | tf_op jit(solution)/shard_map/ppermute | solution.py:56
  642.8 8.1 %collective-permute-start.16 = (bf16[544,384]{0,1:T(8,128)(2,1)S(1)}, bf16[544,384]{0,1:T(8,128)(2,1)S(1)}, u32[]{:S(2)}, u32[]{:S(2)}) collective-permute-start(bf16[544,384]{0,1:T(8,128)(2,1)S(1)} %constant_dynamic-slice_fusion.11), channel_id=1, source_target_pairs={{0,4},{1,5},{2,6},{3,7},{4,0},{5,1},{6,2},{7,3},{8,12},{9,13},{10,... | collective-permute-start | bytes 1253384 | tf_op jit(solution)/shard_map/ppermute | solution.py:56
  651.4 15.5 %collective-permute-start.17 = (bf16[272,384]{0,1:T(8,128)(2,1)S(1)}, bf16[272,384]{0,1:T(8,128)(2,1)S(1)}, u32[]{:S(2)}, u32[]{:S(2)}) collective-permute-start(bf16[272,384]{0,1:T(8,128)(2,1)S(1)} %constant_dynamic-slice_fusion.10), channel_id=1, source_target_pairs={{0,8},{1,9},{2,10},{3,11},{4,12},{5,13},{6,14},{7,15},{8,0},{9,1},... | collective-permute-start | bytes 626696 | tf_op jit(solution)/shard_map/ppermute | solution.py:56
  656.5 78.1 %collective-permute-start.12 = (bf16[1152,384]{0,1:T(8,128)(2,1)}, bf16[1152,384]{0,1:T(8,128)(2,1)}, u32[]{:S(2)}, u32[]{:S(2)}) collective-permute-start(bf16[1152,384]{0,1:T(8,128)(2,1)} %maximum_select_fusion.8), channel_id=1, source_target_pairs={{0,1},{1,0},{2,3},{3,2},{4,5},{5,4},{6,7},{7,6},{8,9},{9,8},{10,11... | collective-permute-start | bytes 2654216 | tf_op jit(solution)/shard_map/ppermute | solution.py:56
  667.1 9.4 %collective-permute-start.18 = (bf16[272,384]{0,1:T(8,128)(2,1)S(1)}, bf16[272,384]{0,1:T(8,128)(2,1)S(1)}, u32[]{:S(2)}, u32[]{:S(2)}) collective-permute-start(bf16[272,384]{0,1:T(8,128)(2,1)S(1)} %add_convert_fusion.10), channel_id=1, source_target_pairs={{0,8},{1,9},{2,10},{3,11},{4,12},{5,13},{6,14},{7,15},{8,0},{9,1},... | collective-permute-start | bytes 626696 | tf_op jit(solution)/shard_map/ppermute | solution.py:56
  677.7 58.7 %collective-permute-start.19 = (bf16[544,384]{0,1:T(8,128)(2,1)}, bf16[544,384]{0,1:T(8,128)(2,1)}, u32[]{:S(2)}, u32[]{:S(2)}) collective-permute-start(bf16[544,384]{0,1:T(8,128)(2,1)} %maximum_select_fusion.15), channel_id=1, source_target_pairs={{0,4},{1,5},{2,6},{3,7},{4,0},{5,1},{6,2},{7,3},{8,12},{9,13},{10,... | collective-permute-start | bytes 1253384 | tf_op jit(solution)/shard_map/ppermute | solution.py:56
  739.8 19.8 %collective-permute-start.20 = (bf16[1088,384]{1,0:T(8,128)(2,1)S(1)}, bf16[1088,384]{1,0:T(8,128)(2,1)}, u32[]{:S(2)}, u32[]{:S(2)}) collective-permute-start(bf16[1088,384]{1,0:T(8,128)(2,1)S(1)} %copy.225), channel_id=1, source_target_pairs={{0,2},{1,3},{2,0},{3,1},{4,6},{5,7},{6,4},{7,5},{8,10},{9,11},{10,... | collective-permute-start | bytes 2506760 | tf_op jit(solution)/shard_map/ppermute | solution.py:56
  763.6 13.7 %collective-permute-start.21 = (bf16[2176,384]{0,1:T(8,128)(2,1)}, bf16[2176,384]{0,1:T(8,128)(2,1)}, u32[]{:S(2)}, u32[]{:S(2)}) collective-permute-start(bf16[2176,384]{0,1:T(8,128)(2,1)} %maximum_select_fusion.4), channel_id=1, source_target_pairs={{0,1},{1,0},{2,3},{3,2},{4,5},{5,4},{6,7},{7,6},{8,9},{9,8},{10,11... | collective-permute-start | bytes 5013512 | tf_op jit(solution)/shard_map/ppermute | solution.py:56
  (73 other events, 546.2 us)
where the time goes:
time: 815 us; the launch traced here: 799 us
  matrix products  270 us (33%)
  local copies, waits for them, and re-layouts  241 us (30%)
  waiting for transfers between devices  104 us (13%)
  other arithmetic  102 us (13%)
  blocking collectives  47.6 us (6%)
  starting transfers between devices  31.5 us (4%)
    unnamed x179, local copies, waits for them, and re-layouts  93.2 us
    ppermute x4, waiting for transfers between devices, swap_group(): return lax.ppermute(field, 'group', [(0, 1), (1, 0)])  69 us
    dot_general x24, matrix products, masked_scores(): jnp.einsum('qd,kd->qk', head_query, head_keys, preferred_element_type=jnp...  53.4 us
    psum x1, blocking collectives, on_device(): gains = lax.psum(gains, ('group', 'replica'))  47.6 us
    dot_general x12, matrix products, forward_head(): jnp.einsum('qk,kd->qd', weights.astype(jnp.bfloat16), head_values, prefer...  41.5 us
    dot_general x4, matrix products, outer(): lax.dot_general(left, right, (((1,), (1,)), ((), ())), preferred_element_...  38.9 us
    ppermute x18, waiting for transfers between devices, swap_replica(): return lax.ppermute(field, 'replica', [(i, i ^ bit) for i in range(count)])  34.6 us
    reshape x16, local copies, waits for them, and re-layouts, unit_of(): parts.append(part[:, i * wide:(i + 1) * wide].reshape(2, rows, wide))  33.3 us
  transfers between devices with their start and end apart: 22, of which 8 were waited for; matrix products, arithmetic and copies ran while one was open for 36% of the time, Pallas kernels for 0%

commit v1 on v0

--- a/solution.py
+++ b/solution.py
@@ -1,3 +1,4 @@
+import functools
 import math
 import jax
 import jax.numpy as jnp
@@ -8,6 +9,14 @@
 HEAD_DIM = 64
 theta_base = 160000.0
 norm_eps = 1e-05
+
+
+def balance_the_works(body, across):
+    r_now = jnp.sum(lax.all_gather(body, across), axis=0)
+    return r_now
+
+
+_wait_members_all = functools.partial(balance_the_works, across=("group", "replica"))
 
 
 def normed(field, gain):
@@ -280,7 +289,7 @@
     grad_down, grad_in, grad_out = spread(early_sum, early)
     (grad_qkv,) = spread(late_sum, late)
     gains = jnp.stack([grad_gain_one, grad_gain_two])
-    gains = lax.psum(gains, ("group", "replica"))
+    gains = _wait_members_all(gains)
     gains = lax.dynamic_slice_in_dim(gains, group * n_own, n_own, 1)
     return (output, grad_tokens, grad_qkv, grad_out, gains[0], grad_in, grad_down, gains[1])
 

time: 815 us -> 754 us (0.925)
  local copies, waits for them, and re-layouts: 241 us -> 206 us
  starting transfers between devices: 31.5 us -> 23.3 us
    psum x1 -> x0, blocking collectives: 47.6 us -> none  [on_device(): gains = lax.psum(gains, ('group', 'replica'))]
    all_gather x0 -> x1, blocking collectives: none -> 46.4 us  [balance_the_works(): r_now = jnp.sum(lax.all_gather(body, across), axis=0)]
    ppermute x4, waiting for transfers between devices: 69 us -> 46.7 us  [swap_group(): return lax.ppermute(field, 'group', [(0, 1), (1, 0)])]
    ppermute x18, waiting for transfers between devices: 34.6 us -> 53.2 us  [swap_replica(): return lax.ppermute(field, 'replica', [(i, i ^ bit) for i in range(count)])]
    dynamic_update_slice x12, local copies, waits for them, and re-layouts: 16.8 us -> 1.32 us  [on_device(): heads, log_totals = lax.map(forward_head, (query, key_rows, values))]
    dynamic_slice x12, local copies, waits for them, and re-layouts: 9.25 us -> 0.16 us  [on_device(): lax.map(backward_head, (query, key_rows, values, d_heads, log_totals))]
    ppermute x18, starting transfers between devices: 26.8 us -> 18.5 us  [swap_replica(): return lax.ppermute(field, 'replica', [(i, i ^ bit) for i in range(count)])]
    unnamed x179 -> x169, local copies, waits for them, and re-layouts: 93.2 us -> 91.6 us
  transfers between devices with their start and end apart: 22 -> 22, of which waited for: 8 -> 9; matrix products, arithmetic and copies ran while one was open for 36% -> 35% of each run, Pallas kernels for 0% -> 0%
where the time goes in v1:
time: 754 us; the launch traced here: 741 us
  matrix products  266 us (35%)
  local copies, waits for them, and re-layouts  206 us (27%)
  waiting for transfers between devices  99.9 us (13%)
  other arithmetic  94.6 us (13%)
  blocking collectives  46.4 us (6%)
  starting transfers between devices  23.3 us (3%)
    unnamed x169, local copies, waits for them, and re-layouts  91.6 us
    dot_general x24, matrix products, masked_scores(): jnp.einsum('qd,kd->qk', head_query, head_keys, preferred_element_type=jnp...  53.4 us
    ppermute x18, waiting for transfers between devices, swap_replica(): return lax.ppermute(field, 'replica', [(i, i ^ bit) for i in range(count)])  53.2 us
    ppermute x4, waiting for transfers between devices, swap_group(): return lax.ppermute(field, 'group', [(0, 1), (1, 0)])  46.7 us
    all_gather x1, blocking collectives, balance_the_works(): r_now = jnp.sum(lax.all_gather(body, across), axis=0)  46.4 us
    dot_general x12, matrix products, forward_head(): jnp.einsum('qk,kd->qd', weights.astype(jnp.bfloat16), head_values, prefer...  41.6 us
    dot_general x4, matrix products, outer(): lax.dot_general(left, right, (((1,), (1,)), ((), ())), preferred_element_...  34.6 us
    reshape x16, local copies, waits for them, and re-layouts, unit_of(): parts.append(part[:, i * wide:(i + 1) * wide].reshape(2, rows, wide))  29.8 us
  transfers between devices with their start and end apart: 22, of which 9 were waited for; matrix products, arithmetic and copies ran while one was open for 35% of the time, Pallas kernels for 0%

profile of v1, /device:TPU:1, one launch (start us, length us, event | category | flops | bytes accessed | tf_op | source)
XLA Modules:
  0.0 740.5 jit_solution(5660760648274779998)
XLA Ops:
  11.8 4.3 copy.179
  34.6 26.8 %collective-permute-done.2 = bf16[2128,384]{1,0:T(8,128)(2,1)} collective-permute-done((bf16[2128,384]{1,0:T(8,128)(2,1)}, bf16[2128,384]{1,0:T(8,128)(2,1)}, u32[]{:S(2)}, u32[]{:S(2)}) %collective-permute-start.2) | collective-permute-done | bytes 1634336 | tf_op jit(solution)/shard_map/ppermute | solution.py:69
  80.1 4.1 convolution_bitcast_fusion
  96.6 4.2 copy.184
  100.8 107.4 %while.30 = (s32[]{:T(128)}, bf16[12,1024,64]{1,2,0:T(8,128)(2,1)S(1)}, f32[12,1024]{1,0:T(8,128)S(1)}, bf16[12,1024,64]{2,1,0:T(8,128)(2,1)}, bf16[12,1024,64]{...) while((s32[]{:T(128)}, bf16[12,1024,64]{1,2,0:T(8,128)(2,1)S(1)}, ...), condition=%wide.region_5.6_spmd.clone.clone, body=%wide.region_2.5_spmd.clone.sunk.clone | while | flops 281018368 | bytes 30455920 | solution.py:187
  230.8 4.3 fusion.87
  235.1 15.0 %fusion.78 = (f32[1024,1152]{1,0:T(8,128)}, f32[1024,1152]{1,0:T(8,128)S(1)}, f32[1024,1152]{1,0:T(8,128)S(1)}) fusion(f32[1024,2304]{1,0:T(8,128)S(1)} %fusion.87, bf16[576,768]{0,1:T(8,128)(2,1)S(1)} %maximum_select_fusion.6, bf16[576,768]{0,1:T(8,128)(2,1)S(1)} %copy-done.41, pred[]{:T(512)S(6)} %eq.18, bf16[1,1024,768]{1,2,0:T(8,128)(2,1)S(1)} %copy-done.8, ...), kind=kOutput, calls=%fused_computation.147 | convolution fusion | flops 1897365504 | bytes 22217728 | tf_op jit(solution)/shard_map/dot_general | solution.py:58
  250.1 4.6 multiply_add_fusion
  254.7 12.1 %multiply_reduce_fusion.1 = (f32[768]{0:T(1024)S(1)}, f32[1024]{0:T(1024)S(1)}, f32[1024,768]{0,1:T(8,128)}) fusion(f32[1024,768]{0,1:T(8,128)S(1)} %copy-done.12, f32[1024]{0:T(1024)S(1)} %fusion.95, f32[1024]{0:T(1024)S(1)} %broadcast_multiply_fusion, f32[768]{0:T(1024)S(1)} %fusion.97, bf16[384,2304]{0,1:T(8,128)(2,1)} %copy-done.29, ...), kind=kOutput, calls=%fused_computation.109 | convolution fusion | flops 3650025728 | bytes 19286016 | tf_op jit(solution)/shard_map/dot_general | solution.py:58
  266.8 9.6 %convolution_convert_fusion = bf16[768,2304]{1,0:T(8,128)(2,1)} fusion(f32[1024,1152]{1,0:T(8,128)} %get-tuple-element.318, f32[1024,1152]{1,0:T(8,128)} %get-tuple-element.312, f32[1024,768]{0,1:T(8,128)S(1)} %copy-done.12, f32[768]{0:T(1024)S(1)} %fusion.97, f32[1024]{0:T(1024)S(1)} %fusion.95, f32[1024]{0:T(1024)S(1)} %broadcast_multiply_fusion), kind=kOutput, calls=%fused_computation.62 | convolution fusion | flops 3633512448 | bytes 16133120 | tf_op jit(solution)/shard_map/dot_general | solution.py:52
  285.7 151.6 %while.31 = (s32[]{:T(128)}, f32[12,1024,64]{1,2,0:T(8,128)}, f32[12,1024,64]{1,2,0:T(8,128)}, bf16[12,1024,64]{1,2,0:T(8,128)(2,1)S(1)}, bf16[12,1024,64]{2,1,0...) while((s32[]{:T(128)}, f32[12,1024,64]{1,2,0:T(8,128)}, ...), condition=%wide.region_12.13_spmd.clone.clone, body=%wide.region_10.12_spmd.clone.sunk.clone | while | flops 681705472 | bytes 34106476 | solution.py:232
  443.1 4.8 convolution_convert_fusion.1
  471.4 6.9 concatenate.218
  501.5 7.1 concatenate.217
  518.0 5.8 collective-permute-done.6
  525.8 6.0 fusion.66
  535.1 18.1 %collective-permute-done.14 = bf16[1,2176,384]{1,2,0:T(8,128)(2,1)S(1)} collective-permute-done((bf16[1,2176,384]{1,2,0:T(8,128)(2,1)S(1)}, bf16[1,2176,384]{1,2,0:T(8,128)(2,1)S(1)}, u32[]{:S(2)}, u32[]{:S(2)}) %collective-permute-start.14) | collective-permute-done | bytes 1671200 | tf_op jit(solution)/shard_map/ppermute | solution.py:69
  558.5 7.4 fusion.79
  569.5 8.5 %collective-permute-done.9 = bf16[144,384]{0,1:T(8,128)(2,1)S(1)} collective-permute-done((bf16[144,384]{0,1:T(8,128)(2,1)S(1)}, bf16[144,384]{0,1:T(8,128)(2,1)S(1)}, u32[]{:S(2)}, u32[]{:S(2)}) %collective-permute-start.9) | collective-permute-done | bytes 110624 | tf_op jit(solution)/shard_map/ppermute | solution.py:65
  588.7 7.9 %collective-permute-done.16 = bf16[544,384]{0,1:T(8,128)(2,1)S(1)} collective-permute-done((bf16[544,384]{0,1:T(8,128)(2,1)S(1)}, bf16[544,384]{0,1:T(8,128)(2,1)S(1)}, u32[]{:S(2)}, u32[]{:S(2)}) %collective-permute-start.16) | collective-permute-done | bytes 417824 | tf_op jit(solution)/shard_map/ppermute | solution.py:65
  602.7 10.1 %collective-permute-done.17 = bf16[272,384]{0,1:T(8,128)(2,1)S(1)} collective-permute-done((bf16[272,384]{0,1:T(8,128)(2,1)S(1)}, bf16[272,384]{0,1:T(8,128)(2,1)S(1)}, u32[]{:S(2)}, u32[]{:S(2)}) %collective-permute-start.17) | collective-permute-done | bytes 208928 | tf_op jit(solution)/shard_map/ppermute | solution.py:65
  621.6 7.7 %collective-permute-done.18 = bf16[272,384]{0,1:T(8,128)(2,1)} collective-permute-done((bf16[272,384]{0,1:T(8,128)(2,1)S(1)}, bf16[272,384]{0,1:T(8,128)(2,1)}, u32[]{:S(2)}, u32[]{:S(2)}) %collective-permute-start.18) | collective-permute-done | bytes 208928 | tf_op jit(solution)/shard_map/ppermute | solution.py:65
  630.7 46.4 %all-gather.1 = f32[32,2,768]{2,1,0:T(2,128)S(1)} all-gather(f32[1,2,768]{2,1,0:T(2,128)S(1)} %maximum_bitcast_fusion), channel_id=2, replica_groups=mesh['group'=2,'replica'=16] {'group','replica'}, dimensions={0}, use_global_device_ids=true | all-gather | bytes 202752 | tf_op jit(solution)/shard_map/all_gather | solution.py:15
  688.8 13.2 %collective-permute-done.20 = bf16[1088,384]{1,0:T(8,128)(2,1)} collective-permute-done((bf16[1088,384]{1,0:T(8,128)(2,1)S(1)}, bf16[1088,384]{1,0:T(8,128)(2,1)}, u32[]{:S(2)}, u32[]{:S(2)}) %collective-permute-start.20) | collective-permute-done | bytes 835616 | tf_op jit(solution)/shard_map/ppermute | solution.py:65
  (518 shorter events, 501.4 us)
Async XLA Ops:
  3.9 26.4 %collective-permute-start = (bf16[400,1152]{1,0:T(8,128)(2,1)}, bf16[400,1152]{1,0:T(8,128)(2,1)}, u32[]{:S(2)}, u32[]{:S(2)}) collective-permute-start(bf16[400,1152]{1,0:T(8,128)(2,1)} %fusion.83), channel_id=1, source_target_pairs={{0,16},{16,0},{1,17},{17,1},{2,18},{18,2},{3,19},{19,3},{4,20},{20... | collective-permute-start | bytes 2764808 | tf_op jit(solution)/shard_map/ppermute | solution.py:69
  10.3 51.1 %collective-permute-start.2 = (bf16[2128,384]{1,0:T(8,128)(2,1)}, bf16[2128,384]{1,0:T(8,128)(2,1)}, u32[]{:S(2)}, u32[]{:S(2)}) collective-permute-start(bf16[2128,384]{1,0:T(8,128)(2,1)} %constant_dynamic-update-slice_fusion), channel_id=1, source_target_pairs={{0,16},{16,0},{1,17},{17,1},{2,18},{18,2},{3,19},{19,3},{4,20},{20... | collective-permute-start | bytes 4902920 | tf_op jit(solution)/shard_map/ppermute | solution.py:69
  25.2 188.4 %copy-start.1 = (bf16[1,1024,768]{1,2,0:T(8,128)(2,1)}, bf16[1,1024,768]{1,2,0:T(8,128)(2,1)S(1)}, u32[]{:S(2)}) copy-start(bf16[1,1024,768]{1,2,0:T(8,128)(2,1)S(1)} %copy.176) | copy-start | bytes 4718596
  30.3 40.1 %collective-permute-start.1 = (bf16[400,1152]{1,0:T(8,128)(2,1)}, bf16[400,1152]{1,0:T(8,128)(2,1)}, u32[]{:S(2)}, u32[]{:S(2)}) collective-permute-start(bf16[400,1152]{1,0:T(8,128)(2,1)} %collective-permute-done), channel_id=1, source_target_pairs={{0,1},{1,0},{2,3},{3,2},{4,5},{5,4},{6,7},{7,6},{8,9},{9,8},{10,11... | collective-permute-start | bytes 2764808 | tf_op jit(solution)/shard_map/ppermute | solution.py:65
  68.5 139.7 %collective-permute-start.3 = (bf16[2128,384]{1,0:T(8,128)(2,1)}, bf16[2128,384]{1,0:T(8,128)(2,1)}, u32[]{:S(2)}, u32[]{:S(2)}) collective-permute-start(bf16[2128,384]{1,0:T(8,128)(2,1)} %collective-permute-done.2), channel_id=1, source_target_pairs={{0,1},{1,0},{2,3},{3,2},{4,5},{5,4},{6,7},{7,6},{8,9},{9,8},{10,11... | collective-permute-start | bytes 4902920 | tf_op jit(solution)/shard_map/ppermute | solution.py:65
  285.7 151.6 %copy-start.35 = (f32[1024,32]{0,1:T(8,128)S(1)}, f32[1024,32]{0,1:T(8,128)}, u32[]{:S(2)}) copy-start(f32[1024,32]{0,1:T(8,128)} %get-tuple-element.382) | copy-start | bytes 393220
  454.0 30.8 %collective-permute-start.4 = (bf16[2,1152,384]{1,2,0:T(8,128)(2,1)}, bf16[2,1152,384]{1,2,0:T(8,128)(2,1)}, u32[]{:S(2)}, u32[]{:S(2)}) collective-permute-start(bf16[2,1152,384]{1,2,0:T(8,128)(2,1)} %pad_maximum_fusion), channel_id=1, source_target_pairs={{0,1},{1,0},{2,3},{3,2},{4,5},{5,4},{6,7},{7,6},{8,9},{9,8},{10,11... | collective-permute-start | bytes 5308424 | tf_op jit(solution)/shard_map/ppermute | solution.py:65
  478.4 35.5 %collective-permute-start.13 = (bf16[2,2176,384]{1,2,0:T(8,128)(2,1)}, bf16[2,2176,384]{1,2,0:T(8,128)(2,1)}, u32[]{:S(2)}, u32[]{:S(2)}) collective-permute-start(bf16[2,2176,384]{1,2,0:T(8,128)(2,1)} %concatenate.218), channel_id=1, source_target_pairs={{0,1},{1,0},{2,3},{3,2},{4,5},{5,4},{6,7},{7,6},{8,9},{9,8},{10,11... | collective-permute-start | bytes 10027016 | tf_op jit(solution)/shard_map/ppermute | solution.py:65
  489.3 21.0 %collective-permute-start.5 = (bf16[1,1152,384]{1,2,0:T(8,128)(2,1)}, bf16[1,1152,384]{1,2,0:T(8,128)(2,1)}, u32[]{:S(2)}, u32[]{:S(2)}) collective-permute-start(bf16[1,1152,384]{1,2,0:T(8,128)(2,1)} %constant_dynamic-slice_fusion.22), channel_id=1, source_target_pairs={{0,16},{16,0},{1,17},{17,1},{2,18},{18,2},{3,19},{19,3},{4,20},{20... | collective-permute-start | bytes 2654216 | tf_op jit(solution)/shard_map/ppermute | solution.py:69
  512.3 11.6 %collective-permute-start.6 = (bf16[576,384]{0,1:T(8,128)(2,1)S(1)}, bf16[576,384]{0,1:T(8,128)(2,1)S(1)}, u32[]{:S(2)}, u32[]{:S(2)}) collective-permute-start(bf16[576,384]{0,1:T(8,128)(2,1)S(1)} %dynamic-slice_bitcast_fusion), channel_id=1, source_target_pairs={{0,2},{1,3},{2,0},{3,1},{4,6},{5,7},{6,4},{7,5},{8,10},{9,11},{10,... | collective-permute-start | bytes 1327112 | tf_op jit(solution)/shard_map/ppermute | solution.py:65
  516.7 36.5 %collective-permute-start.14 = (bf16[1,2176,384]{1,2,0:T(8,128)(2,1)S(1)}, bf16[1,2176,384]{1,2,0:T(8,128)(2,1)S(1)}, u32[]{:S(2)}, u32[]{:S(2)}) collective-permute-start(bf16[1,2176,384]{1,2,0:T(8,128)(2,1)S(1)} %constant_dynamic-slice_fusion.13), channel_id=1, source_target_pairs={{0,16},{16,0},{1,17},{17,1},{2,18},{18,2},{3,19},{19,3},{4,20},{20... | collective-permute-start | bytes 5013512 | tf_op jit(solution)/shard_map/ppermute | solution.py:69
  524.3 7.6 %collective-permute-start.7 = (bf16[288,384]{0,1:T(8,128)(2,1)S(1)}, bf16[288,384]{0,1:T(8,128)(2,1)S(1)}, u32[]{:S(2)}, u32[]{:S(2)}) collective-permute-start(bf16[288,384]{0,1:T(8,128)(2,1)S(1)} %constant_dynamic-slice_fusion.21), channel_id=1, source_target_pairs={{0,4},{1,5},{2,6},{3,7},{4,0},{5,1},{6,2},{7,3},{8,12},{9,13},{10,... | collective-permute-start | bytes 663560 | tf_op jit(solution)/shard_map/ppermute | solution.py:65
  532.8 33.1 %collective-permute-start.8 = (bf16[144,384]{0,1:T(8,128)(2,1)}, bf16[144,384]{0,1:T(8,128)(2,1)}, u32[]{:S(2)}, u32[]{:S(2)}) collective-permute-start(bf16[144,384]{0,1:T(8,128)(2,1)} %constant_dynamic-slice_fusion.20), channel_id=1, source_target_pairs={{0,8},{1,9},{2,10},{3,11},{4,12},{5,13},{6,14},{7,15},{8,0},{9,1},... | collective-permute-start | bytes 331784 | tf_op jit(solution)/shard_map/ppermute | solution.py:65
  558.3 20.3 %collective-permute-start.15 = (bf16[1088,384]{1,0:T(8,128)(2,1)}, bf16[1088,384]{1,0:T(8,128)(2,1)}, u32[]{:S(2)}, u32[]{:S(2)}) collective-permute-start(bf16[1088,384]{1,0:T(8,128)(2,1)} %bitcast.247), channel_id=1, source_target_pairs={{0,2},{1,3},{2,0},{3,1},{4,6},{5,7},{6,4},{7,5},{8,10},{9,11},{10,... | collective-permute-start | bytes 2506760 | tf_op jit(solution)/shard_map/ppermute | solution.py:65
  567.0 11.0 %collective-permute-start.9 = (bf16[144,384]{0,1:T(8,128)(2,1)S(1)}, bf16[144,384]{0,1:T(8,128)(2,1)S(1)}, u32[]{:S(2)}, u32[]{:S(2)}) collective-permute-start(bf16[144,384]{0,1:T(8,128)(2,1)S(1)} %add_convert_fusion.12), channel_id=1, source_target_pairs={{0,8},{1,9},{2,10},{3,11},{4,12},{5,13},{6,14},{7,15},{8,0},{9,1},... | collective-permute-start | bytes 331784 | tf_op jit(solution)/shard_map/ppermute | solution.py:65
  578.3 7.7 %collective-permute-start.10 = (bf16[288,384]{0,1:T(8,128)(2,1)S(1)}, bf16[288,384]{0,1:T(8,128)(2,1)}, u32[]{:S(2)}, u32[]{:S(2)}) collective-permute-start(bf16[288,384]{0,1:T(8,128)(2,1)S(1)} %maximum_select_fusion.16), channel_id=1, source_target_pairs={{0,4},{1,5},{2,6},{3,7},{4,0},{5,1},{6,2},{7,3},{8,12},{9,13},{10,... | collective-permute-start | bytes 663560 | tf_op jit(solution)/shard_map/ppermute | solution.py:65
  583.3 13.3 %collective-permute-start.16 = (bf16[544,384]{0,1:T(8,128)(2,1)S(1)}, bf16[544,384]{0,1:T(8,128)(2,1)S(1)}, u32[]{:S(2)}, u32[]{:S(2)}) collective-permute-start(bf16[544,384]{0,1:T(8,128)(2,1)S(1)} %constant_dynamic-slice_fusion.11), channel_id=1, source_target_pairs={{0,4},{1,5},{2,6},{3,7},{4,0},{5,1},{6,2},{7,3},{8,12},{9,13},{10,... | collective-permute-start | bytes 1253384 | tf_op jit(solution)/shard_map/ppermute | solution.py:65
  587.5 10.6 %collective-permute-start.11 = (bf16[576,384]{0,1:T(8,128)(2,1)S(1)}, bf16[576,384]{0,1:T(8,128)(2,1)S(1)}, u32[]{:S(2)}, u32[]{:S(2)}) collective-permute-start(bf16[576,384]{0,1:T(8,128)(2,1)S(1)} %maximum_select_fusion.14), channel_id=1, source_target_pairs={{0,2},{1,3},{2,0},{3,1},{4,6},{5,7},{6,4},{7,5},{8,10},{9,11},{10,... | collective-permute-start | bytes 1327112 | tf_op jit(solution)/shard_map/ppermute | solution.py:65
  597.1 15.7 %collective-permute-start.17 = (bf16[272,384]{0,1:T(8,128)(2,1)S(1)}, bf16[272,384]{0,1:T(8,128)(2,1)S(1)}, u32[]{:S(2)}, u32[]{:S(2)}) collective-permute-start(bf16[272,384]{0,1:T(8,128)(2,1)S(1)} %constant_dynamic-slice_fusion.10), channel_id=1, source_target_pairs={{0,8},{1,9},{2,10},{3,11},{4,12},{5,13},{6,14},{7,15},{8,0},{9,1},... | collective-permute-start | bytes 626696 | tf_op jit(solution)/shard_map/ppermute | solution.py:65
  599.6 78.3 %collective-permute-start.12 = (bf16[1152,384]{0,1:T(8,128)(2,1)}, bf16[1152,384]{0,1:T(8,128)(2,1)}, u32[]{:S(2)}, u32[]{:S(2)}) collective-permute-start(bf16[1152,384]{0,1:T(8,128)(2,1)} %maximum_select_fusion.8), channel_id=1, source_target_pairs={{0,1},{1,0},{2,3},{3,2},{4,5},{5,4},{6,7},{7,6},{8,9},{9,8},{10,11... | collective-permute-start | bytes 2654216 | tf_op jit(solution)/shard_map/ppermute | solution.py:65
  613.0 16.3 %collective-permute-start.18 = (bf16[272,384]{0,1:T(8,128)(2,1)S(1)}, bf16[272,384]{0,1:T(8,128)(2,1)}, u32[]{:S(2)}, u32[]{:S(2)}) collective-permute-start(bf16[272,384]{0,1:T(8,128)(2,1)S(1)} %add_convert_fusion.10), channel_id=1, source_target_pairs={{0,8},{1,9},{2,10},{3,11},{4,12},{5,13},{6,14},{7,15},{8,0},{9,1},... | collective-permute-start | bytes 626696 | tf_op jit(solution)/shard_map/ppermute | solution.py:65
  630.6 49.0 %collective-permute-start.19 = (bf16[544,384]{0,1:T(8,128)(2,1)S(1)}, bf16[544,384]{0,1:T(8,128)(2,1)S(1)}, u32[]{:S(2)}, u32[]{:S(2)}) collective-permute-start(bf16[544,384]{0,1:T(8,128)(2,1)S(1)} %maximum_select_fusion.15), channel_id=1, source_target_pairs={{0,4},{1,5},{2,6},{3,7},{4,0},{5,1},{6,2},{7,3},{8,12},{9,13},{10,... | collective-permute-start | bytes 1253384 | tf_op jit(solution)/shard_map/ppermute | solution.py:65
  681.8 20.2 %collective-permute-start.20 = (bf16[1088,384]{1,0:T(8,128)(2,1)S(1)}, bf16[1088,384]{1,0:T(8,128)(2,1)}, u32[]{:S(2)}, u32[]{:S(2)}) collective-permute-start(bf16[1088,384]{1,0:T(8,128)(2,1)S(1)} %copy.225), channel_id=1, source_target_pairs={{0,2},{1,3},{2,0},{3,1},{4,6},{5,7},{6,4},{7,5},{8,10},{9,11},{10,... | collective-permute-start | bytes 2506760 | tf_op jit(solution)/shard_map/ppermute | solution.py:65
  706.0 12.8 %collective-permute-start.21 = (bf16[2176,384]{0,1:T(8,128)(2,1)}, bf16[2176,384]{0,1:T(8,128)(2,1)}, u32[]{:S(2)}, u32[]{:S(2)}) collective-permute-start(bf16[2176,384]{0,1:T(8,128)(2,1)} %maximum_select_fusion.4), channel_id=1, source_target_pairs={{0,1},{1,0},{2,3},{3,2},{4,5},{5,4},{6,7},{7,6},{8,9},{9,8},{10,11... | collective-permute-start | bytes 5013512 | tf_op jit(solution)/shard_map/ppermute | solution.py:65
  (68 other events, 624.5 us)
